TPU v7x, 32 devices: a whole 2x2x4 slice. The times are simulated.
32 devices in a mesh: group: 2 (over x), dom: 16 (over z, y, core).
Axes of the slice: x: 2, y: 2, z: 4, core: 2. Of those that a mesh axis runs over, the one named last changes fastest.
Arguments:
- features: bfloat16 [8192, 512], P(('group', 'dom')), may hold values from -6 to 6
- tile_columns: int32 [32, 2, 4], P(('group', 'dom')), may hold values from 0 to 1
- tile_values: bfloat16 [32, 2, 4, 128, 128], P(('group', 'dom')), as said below
- send_rows: int32 [32, 16, 16], P(('group', 'dom')), may hold values from 0 to 255
- send_count: int32 [32, 16], P(('group', 'dom')), may hold values from 0 to 16, as said below
- ghost_target: int32 [32, 16, 16], P(('group', 'dom')), may hold values from 0 to 255
- query_rows: int32 [32, 512], P(('group', 'dom')), may hold values from 0 to 255
- positive_cand: int32 [32, 512], P(('group', 'dom')), may hold values from 0 to 63
- negative_rows: int32 [32, 32], P(('group', 'dom')), may hold values from 0 to 255
- weight_self: bfloat16 [512, 512], replicated, may hold values from -0.25 to 0.25
- weight_neigh: bfloat16 [512, 512], replicated, may hold values from -0.75 to 0.75
Outputs:
- embeddings: bfloat16 [8192, 512], P(('group', 'dom'))
- weight_grads: bfloat16 [1024, 512], P('dom')
Inputs may be any that keep to these rules, and one draw needn't show every extreme that they name: `send_count`: no device sends rows to its own index of dom; in every group one index of dom receives exactly 16 rows from every other index. `tile_values`: weights are zero or between 0.5 and 1.
All inputs are finite; a program needn't handle non-finite values.
Results may differ from a plain program's by a relative error of at most 0.015.
Values may be sent and summed in bfloat16 or wider, within the bound.
No kernel may reach another device: no remote copies, remote signals or barrier semaphores. Data moves between devices by JAX's collectives and lax.ppermute only.
A program may use at most 64 MiB of HBM per device.

v0:
```python
import math
import jax
import jax.numpy as jnp
from jax import lax
from jax.sharding import PartitionSpec as P

LOSS_FACTOR = 64.0
EPSILON = 1e-05


def score_grads(scores, positive, cand_total, query_total):
    sigma = jax.nn.sigmoid(scores)
    dscore = jnp.where(positive, sigma - 1.0, sigma / (cand_total - 1.0)) * (
        LOSS_FACTOR / query_total
    )
    return dscore.astype(jnp.bfloat16)


def transpose_dot(left, right):
    return lax.dot_general(
        left, right, (((0,), (0,)), ((), ())), preferred_element_type=jnp.float32
    )


def on_device(
    features,
    tile_columns,
    tile_values,
    send_rows,
    send_count,
    ghost_target,
    query_rows,
    positive_cand,
    negative_rows,
    weight_self,
    weight_neigh,
):
    node_count, width = features.shape
    row_blocks, tiles_row, tile_size = (
        tile_values.shape[1],
        tile_values.shape[2],
        tile_values.shape[3],
    )
    slot_count = send_rows.shape[2]
    group_count = lax.axis_size("group")
    score_factor = 1.0 / math.sqrt(width)
    outgoing = features[send_rows[0]]
    flags = (jnp.arange(slot_count, dtype=jnp.int32)[None, :] < send_count[0][:, None]).astype(
        jnp.bfloat16
    )
    received, flags_in = (
        lax.all_to_all(outgoing, "dom", split_axis=0, concat_axis=0, tiled=True),
        lax.all_to_all(flags, "dom", split_axis=0, concat_axis=0, tiled=True),
    )
    blocks = features.reshape(row_blocks, tile_size, width)
    picked = blocks[tile_columns[0]]
    local = jnp.einsum(
        "rtij,rtjd->rid", tile_values[0], picked, preferred_element_type=jnp.float32
    ).reshape(node_count, width)
    row_weight = jnp.sum(tile_values[0].astype(jnp.float32), axis=(1, 3)).reshape(node_count)
    live = flags_in.astype(jnp.float32)
    targets = ghost_target[0].reshape(-1)
    weighted = (received.astype(jnp.float32) * live[:, :, None]).reshape(-1, width)
    ghost_sum = jnp.zeros((node_count, width), jnp.float32).at[targets].add(weighted)
    ghost_count = jnp.zeros((node_count,), jnp.float32).at[targets].add(live.reshape(-1))
    degree = 1.0 + row_weight + ghost_count
    aggregate = ((local + ghost_sum) / degree[:, None]).astype(jnp.bfloat16)
    pre = jnp.dot(features, weight_self, preferred_element_type=jnp.float32) + jnp.dot(
        aggregate, weight_neigh, preferred_element_type=jnp.float32
    )
    scale = lax.rsqrt(jnp.mean(pre * pre, axis=-1, keepdims=True) + EPSILON)
    embeds = (pre * scale).astype(jnp.bfloat16)
    queries = embeds[query_rows[0]]
    own_negs = embeds[negative_rows[0]]
    neg_count = own_negs.shape[0]
    query_total = queries.shape[0]
    cand_total = neg_count * group_count
    targets_pos = positive_cand[0][:, None]
    all_negs = lax.all_gather(own_negs, "group", axis=0, tiled=True)
    scores = score_factor * jnp.dot(queries, all_negs.T, preferred_element_type=jnp.float32)
    positive = targets_pos == jnp.arange(cand_total, dtype=jnp.int32)[None, :]
    dscore = score_grads(scores, positive, cand_total, query_total)
    query_grad = score_factor * jnp.dot(dscore, all_negs, preferred_element_type=jnp.float32)
    neg_grad = lax.psum_scatter(
        (score_factor * transpose_dot(dscore, queries)).astype(jnp.bfloat16),
        "group",
        scatter_dimension=0,
        tiled=True,
    ).astype(jnp.float32)
    emb_grad = jnp.zeros((node_count, width), jnp.float32)
    emb_grad = emb_grad.at[query_rows[0]].add(query_grad)
    emb_grad = emb_grad.at[negative_rows[0]].add(neg_grad)
    inner = jnp.mean(pre * emb_grad, axis=-1, keepdims=True)
    pre_grad = (scale * emb_grad - pre * scale * scale * scale * inner).astype(jnp.bfloat16)
    stacked = jnp.concatenate([features, aggregate], axis=1)
    shard = lax.psum_scatter(
        transpose_dot(stacked, pre_grad), "dom", scatter_dimension=0, tiled=True
    )
    summed = lax.psum(shard.astype(jnp.bfloat16), "group")
    return (embeds, summed)


def solution(mesh):
    placed = (
        P(("group", "dom"), None),
        P(("group", "dom"), None, None),
        P(("group", "dom"), None, None, None, None),
        P(("group", "dom"), None, None),
        P(("group", "dom"), None),
        P(("group", "dom"), None, None),
        P(("group", "dom"), None),
        P(("group", "dom"), None),
        P(("group", "dom"), None),
        P(),
        P(),
    )
    return jax.shard_map(
        on_device,
        mesh=mesh,
        in_specs=placed,
        out_specs=(P(("group", "dom"), None), P("dom", None)),
        check_vma=False,
    )
```

profile of v0, /device:TPU:0, one launch (start us, length us, event | category | flops | bytes accessed | tf_op | source)
XLA Modules:
  0.0 157.0 jit_solution(12821754926774188139)
XLA Ops:
  7.2 0.0 copy-start
  7.2 0.0 copy-start.2
  7.2 1.4 compare_convert_fusion
  8.6 7.4 %all-to-all-start.1 = ((bf16[16,1,16]{2,1,0:T(2,128)(2,1)}), bf16[16,1,16]{2,1,0:T(2,128)(2,1)S(1)}, u32[]{:S(2)}, u32[]{:S(2)}) async-start(bf16[16,1,16]{2,1,0:T(2,128)(2,1)} %compare_convert_fusion), calls=%async_computation.1 | async-start | bytes 16384 | tf_op jit(solution)/shard_map/all_to_all | solution.py:53
  16.0 0.7 fusion.17
  16.7 0.7 compare_select_fusion.3
  17.4 0.1 reshape.231
  17.4 0.8 reshape_squeeze.3
  18.2 1.1 convert_reduce_fusion
  19.3 0.7 compare_select_fusion.1
  20.0 0.7 compare_select_fusion
  20.7 0.1 reshape.239
  20.8 1.4 fusion.19
  22.2 0.0 copy-done.2
  22.3 0.0 copy-start.3
  22.3 1.9 %gather_fusion.1 = bf16[256,512]{1,0:T(8,128)(2,1)} fusion(bf16[256,512]{1,0:T(8,128)(2,1)S(1)} %copy-done.2, s32[1024]{0:T(1024)S(1)} %pad_clamp_fusion.2), kind=kCustom, calls=%fused_computation.1 | custom fusion | bytes 525312 | tf_op jit(solution)/shard_map/gather | solution.py:47
  24.1 0.6 gather_fusion
  24.7 0.0 all-to-all-done.1
  24.8 6.0 %all-to-all-start = ((bf16[16,16,512]{2,1,0:T(8,128)(2,1)}), bf16[16,16,512]{2,1,0:T(8,128)(2,1)S(1)}, u32[]{:S(2)}, u32[]{:S(2)}) async-start(bf16[16,16,512]{2,1,0:T(8,128)(2,1)} %bitcast.10), calls=%async_computation | async-start | bytes 524288 | tf_op jit(solution)/shard_map/all_to_all | solution.py:52
  30.8 0.0 reduce-scatter.3.cloned.1.call-start
  30.8 0.0 copy-done.3
  30.9 0.3 fusion.9
  31.2 0.1 reshape.273
  31.3 2.3 %scatter_fusion.1 = f32[256]{0:T(256)S(1)} fusion(f32[256]{0:T(256)S(1)} %add_bitcast_fusion, s32[256]{0:T(256)S(1)} %bitcast.51, f32[256]{0:T(256)S(1)} %reshape.273), kind=kCustom, calls=%fused_computation.5 | custom fusion | flops 256 | bytes 4096 | tf_op jit(solution)/shard_map/scatter-add | solution.py:65
  33.6 7.2 %all-to-all-done = bf16[16,16,512]{2,1,0:T(8,128)(2,1)S(1)} async-done(((bf16[16,16,512]{2,1,0:T(8,128)(2,1)}), bf16[16,16,512]{2,1,0:T(8,128)(2,1)S(1)}, u32[]{:S(2)}, u32[]{:S(2)}) %all-to-all-start) | async-done | bytes 262176 | tf_op jit(solution)/shard_map/all_to_all | solution.py:52
  40.8 0.1 convert_multiply_fusion
  40.9 2.3 %scatter_fusion = f32[256,512]{1,0:T(8,128)S(1)} fusion(f32[256,512]{1,0:T(8,128)S(1)} %bitcast.46, s32[256]{0:T(256)S(1)} %bitcast.52, f32[256,512]{1,0:T(8,128)S(1)} %bitcast.49), kind=kCustom, calls=%fused_computation.4 | custom fusion | flops 131072 | bytes 1573888 | tf_op jit(solution)/shard_map/scatter-add | solution.py:64
  43.2 0.1 divide_convert_fusion
  43.3 0.0 copy-done
  43.3 0.4 multiply_reduce_fusion.1
  43.7 0.1 multiply_convert_fusion
  43.9 0.0 copy-start.1
  43.9 0.6 gather_fusion.3
  44.5 4.6 %all-gather = bf16[64,512]{1,0:T(8,128)(2,1)S(1)} all-gather(bf16[32,512]{1,0:T(8,128)(2,1)S(1)} %gather_fusion.3), channel_id=2, replica_groups=mesh['group'=2,'dom'=16] {'group'}, dimensions={0}, use_global_device_ids=true | all-gather | bytes 98304 | tf_op jit(solution)/shard_map/all_gather | solution.py:79
  49.1 0.0 copy-start.4
  49.1 2.0 %gather_fusion.2 = bf16[512,512]{1,0:T(8,128)(2,1)S(1)} fusion(bf16[256,512]{1,0:T(8,128)(2,1)S(1)} %multiply_convert_fusion, s32[1024]{0:T(1024)S(1)} %pad_clamp_fusion.1), kind=kCustom, calls=%fused_computation.2 | custom fusion | bytes 1050624 | tf_op jit(solution)/shard_map/gather | solution.py:73
  51.1 0.0 copy-done.1
  51.1 0.0 copy-done.4
  51.1 0.3 multiply_convert_fusion.1
  51.4 0.8 fusion.4
  52.3 0.0 reduce-scatter.3.cloned.1.call-update
  52.3 0.0 reduce-scatter.5.cloned.1.call-start
  52.3 0.3 convolution_multiply_fusion
  52.6 3.7 %scatter_custom_fusion.2 = f32[256,512]{1,0:T(8,128)S(1)} fusion(s32[512]{0:T(512)S(1)} %bitcast.54, f32[512,512]{1,0:T(8,128)S(1)} %convolution_multiply_fusion, f32[]{:T(128)} %constant.14.clone.1), kind=kCustom, calls=%fused_computation.31 | custom fusion | flops 262144 | bytes 524292 | tf_op jit(solution)/shard_map/scatter-add | solution.py:91
  56.4 4.3 %reduce-scatter.3.cloned.1.call-done = bf16[32,512]{1,0:T(8,128)(2,1)} async-done(((bf16[64,512]{1,0:T(8,128)(2,1)}), bf16[32,512]{1,0:T(8,128)(2,1)}) %reduce-scatter.3.cloned.1.call-update) | async-done | bytes 32784 | tf_op jit(solution)/shard_map/reduce_scatter | solution.py:84
  60.6 1.2 scatter_custom_fusion.3
  61.9 0.1 multiply_reduce_fusion
  62.0 2.0 %fusion.5 = f32[1024,512]{1,0:T(8,128)} fusion(bf16[256,512]{1,0:T(8,128)(2,1)S(1)} %divide_convert_fusion, bf16[256,512]{1,0:T(8,128)(2,1)S(1)} %copy-done.2, f32[256,512]{1,0:T(8,128)S(1)} %scatter_custom_fusion.3, f32[256,512]{1,0:T(8,128)S(1)} %get-tuple-element.3, f32[256]{0:T(256)S(1)} %broadcast_multiply_fusion, f32[256]{0:T(256)S(1)} %add_rsqrt_fusion), kind=kOutput, calls=%fused_computation.17 | convolution fusion | flops 270401536 | bytes 3672064 | tf_op jit(solution)/shard_map/dot_general | solution.py:20
  64.0 0.0 reduce-scatter.5.cloned.1.call-update
  64.0 0.0 all-reduce.2.cloned.1.call-start
  64.0 62.2 %reduce-scatter.5.cloned.1.call-done = f32[64,512]{1,0:T(8,128)} async-done(((f32[1024,512]{1,0:T(8,128)}), f32[64,512]{1,0:T(8,128)}) %reduce-scatter.5.cloned.1.call-update) | async-done | bytes 131088 | tf_op jit(solution)/shard_map/reduce_scatter | solution.py:96
  126.2 1.5 convert_element_type.66
  127.8 0.0 all-reduce.2.cloned.1.call-update
  127.8 21.2 %all-reduce.2.cloned.1.call-done = bf16[64,512]{1,0:T(8,128)(2,1)} async-done(((bf16[64,512]{1,0:T(8,128)(2,1)}), bf16[64,512]{1,0:T(8,128)(2,1)}) %all-reduce.2.cloned.1.call-update) | async-done | bytes 65552 | tf_op jit(solution)/shard_map/psum | solution.py:99
  149.0 1.5 copy.18
  (10 shorter events, 0.1 us)
Async XLA Ops:
  7.2 36.2 %copy-start = (bf16[512,512]{1,0:T(8,128)(2,1)S(1)}, bf16[512,512]{1,0:T(8,128)(2,1)}, u32[]{:S(2)}) copy-start(bf16[512,512]{1,0:T(8,128)(2,1)} %param.21) | copy-start | bytes 1572868
  7.2 15.1 %copy-start.2 = (bf16[256,512]{1,0:T(8,128)(2,1)S(1)}, bf16[256,512]{1,0:T(8,128)(2,1)}, u32[]{:S(2)}) copy-start(bf16[256,512]{1,0:T(8,128)(2,1)} %param.11) | copy-start | bytes 786436
  8.6 16.1 %all-to-all-start.1 = ((bf16[16,1,16]{2,1,0:T(2,128)(2,1)}), bf16[16,1,16]{2,1,0:T(2,128)(2,1)S(1)}, u32[]{:S(2)}, u32[]{:S(2)}) async-start(bf16[16,1,16]{2,1,0:T(2,128)(2,1)} %compare_convert_fusion), calls=%async_computation.1 | async-start | bytes 16384 | tf_op jit(solution)/shard_map/all_to_all | solution.py:53
  22.3 8.6 %copy-start.3 = (bf16[1,2,4,128,128]{4,3,2,1,0:T(8,128)(2,1)S(1)}, bf16[1,2,4,128,128]{4,3,2,1,0:T(8,128)(2,1)}, u32[]{:S(2)}) copy-start(bf16[1,2,4,128,128]{4,3,2,1,0:T(8,128)(2,1)} %param.13) | copy-start | bytes 786436
  24.8 16.0 %all-to-all-start = ((bf16[16,16,512]{2,1,0:T(8,128)(2,1)}), bf16[16,16,512]{2,1,0:T(8,128)(2,1)S(1)}, u32[]{:S(2)}, u32[]{:S(2)}) async-start(bf16[16,16,512]{2,1,0:T(8,128)(2,1)} %bitcast.10), calls=%async_computation | async-start | bytes 524288 | tf_op jit(solution)/shard_map/all_to_all | solution.py:52
  30.8 29.9 %reduce-scatter.3.cloned.1.call-start = ((), (), s32[]{:S(2)}) async-start(), calls=%async_computation.4 | async-start | bytes 98304 | tf_op jit(solution)/shard_map/reduce_scatter | solution.py:84
  43.9 7.2 %copy-start.1 = (bf16[256,512]{1,0:T(8,128)(2,1)}, bf16[256,512]{1,0:T(8,128)(2,1)S(1)}, u32[]{:S(2)}) copy-start(bf16[256,512]{1,0:T(8,128)(2,1)S(1)} %multiply_convert_fusion) | copy-start | bytes 786436
  49.1 2.0 %copy-start.4 = (s32[1,512]{1,0:T(1,128)S(1)}, s32[1,512]{1,0:T(1,128)}, u32[]{:S(2)}) copy-start(s32[1,512]{1,0:T(1,128)} %param.18) | copy-start | bytes 6148
  52.3 74.0 %reduce-scatter.5.cloned.1.call-start = ((), (), s32[]{:S(2)}) async-start(), calls=%async_computation.5 | async-start | bytes 2228224 | tf_op jit(solution)/shard_map/reduce_scatter | solution.py:96
  64.0 85.0 %all-reduce.2.cloned.1.call-start = ((), (), s32[]{:S(2)}) async-start(), calls=%async_computation.6 | async-start | bytes 131072 | tf_op jit(solution)/shard_map/psum | solution.py:99
Sparse Core Ops, SparseCore 0:
  52.4 8.1 reduce-scatter.2
  64.4 61.8 reduce-scatter.4
  129.1 19.8 all-reduce.1
where the time goes:
time: 158 us; the launch traced here: 157 us
  waiting for transfers between devices  94.9 us (60%)
  other arithmetic  16.8 us (11%)
  between operations  14 us (9%)
  starting transfers between devices  13.6 us (9%)
  local copies, waits for them, and re-layouts  7.58 us (5%)
  matrix products  5.54 us (4%)
  blocking collectives  4.58 us (3%)
    reduce_scatter x1, waiting for transfers between devices, on_device(): lax.psum_scatter(transpose_dot(stacked, pre_grad), 'dom', scatter_dimensi...  62.2 us
    psum x1, waiting for transfers between devices, on_device(): summed = lax.psum(shard.astype(jnp.bfloat16), 'group')  21.2 us
    all_to_all x1, starting transfers between devices, on_device(): lax.all_to_all(flags, 'dom', split_axis=0, concat_axis=0, tiled=True)  7.41 us
    all_to_all x1, waiting for transfers between devices, on_device(): lax.all_to_all(outgoing, 'dom', split_axis=0, concat_axis=0, tiled=True)  7.18 us
    all_to_all x1, starting transfers between devices, on_device(): lax.all_to_all(outgoing, 'dom', split_axis=0, concat_axis=0, tiled=True)  6.02 us
    all_gather x1, blocking collectives, on_device(): all_negs = lax.all_gather(own_negs, 'group', axis=0, tiled=True)  4.58 us
    reduce_scatter x1, waiting for transfers between devices, on_device(): lax.psum_scatter((score_factor * transpose_dot(dscore, queries)).astype(j...  4.28 us
    scatter-add x1, other arithmetic, on_device(): emb_grad = emb_grad.at[query_rows[0]].add(query_grad)  3.71 us
  transfers between devices with their start and end apart: 5, of which 4 were waited for; matrix products, arithmetic and copies ran while one was open for 10% of the time, Pallas kernels for 0%

commit v1 on v0

--- a/solution.py
+++ b/solution.py
@@ -1,3 +1,4 @@
+import functools
 import math
 import jax
 import jax.numpy as jnp
@@ -6,6 +7,43 @@
 
 LOSS_FACTOR = 64.0
 EPSILON = 1e-05
+
+
+def build_tracks(frame_in, out_dim, buf):
+    g_now = frame_in.shape
+    field_out = frame_in.reshape(
+        *g_now[:out_dim], buf, g_now[out_dim] // buf, *g_now[out_dim + 1 :]
+    )
+    shaped = jnp.moveaxis(field_out, out_dim, 0)
+    return shaped
+
+
+def produce_islands(frame, array_dim):
+    frame = jnp.moveaxis(frame, 0, array_dim)
+    current_value = frame.shape
+    tile_out = frame.reshape(
+        *current_value[:array_dim],
+        current_value[array_dim] * current_value[array_dim + 1],
+        *current_value[array_dim + 2 :]
+    )
+    return tile_out
+
+
+def return_all_the_matrix(payload, row_axis, inputs, s0):
+    y2 = jax.lax.axis_size(row_axis)
+    v1, all_values = (y2, jax.lax.axis_index(row_axis))
+    local_now = build_tracks(payload, inputs, v1)
+    a_now = local_now
+    for it in range(1, v1):
+        s_next, lower = ((all_values + it) % v1, (all_values - it) % v1)
+        seen_now = lax.dynamic_index_in_dim(local_now, s_next, 0)
+        built = jax.lax.ppermute(seen_now, row_axis, [(dd, (dd + it) % v1) for dd in range(v1)])
+        a_now = lax.dynamic_update_slice_in_dim(a_now, built, lower, axis=0)
+    h_now = produce_islands(a_now, s0)
+    return h_now
+
+
+process_map = functools.partial(return_all_the_matrix, row_axis="dom", inputs=0, s0=0)
 
 
 def score_grads(scores, positive, cand_total, query_total):
@@ -49,7 +87,7 @@
         jnp.bfloat16
     )
     received, flags_in = (
-        lax.all_to_all(outgoing, "dom", split_axis=0, concat_axis=0, tiled=True),
+        process_map(outgoing),
         lax.all_to_all(flags, "dom", split_axis=0, concat_axis=0, tiled=True),
     )
     blocks = features.reshape(row_blocks, tile_size, width)

time: 158 us -> 196 us (1.24)
  waiting for transfers between devices: 94.9 us -> 130 us
  starting transfers between devices: 13.6 us -> 20.3 us
  other arithmetic: 16.8 us -> 13.9 us
    ppermute x0 -> x15, waiting for transfers between devices: none -> 38.3 us  [return_all_the_matrix(): jax.lax.ppermute(seen_now, row_axis, [(dd, (dd + it) % v1) for dd in rang...]
    ppermute x0 -> x15, starting transfers between devices: none -> 12.7 us  [return_all_the_matrix(): jax.lax.ppermute(seen_now, row_axis, [(dd, (dd + it) % v1) for dd in rang...]
    all_to_all x1 -> x0, waiting for transfers between devices: 7.18 us -> none  [on_device(): lax.all_to_all(outgoing, 'dom', split_axis=0, concat_axis=0, tiled=True)]
    all_to_all x1 -> x0, starting transfers between devices: 6.02 us -> none  [on_device(): lax.all_to_all(outgoing, 'dom', split_axis=0, concat_axis=0, tiled=True)]
    reduce_scatter x1, waiting for transfers between devices: 4.28 us -> 8.53 us  [on_device(): lax.psum_scatter((score_factor * transpose_dot(dscore, queries)).astype(j...]
  transfers between devices with their start and end apart: 5 -> 19, of which waited for: 4 -> 13; matrix products, arithmetic and copies ran while one was open for 10% -> 6% of each run, Pallas kernels for 0% -> 0%
where the time goes in v1:
time: 196 us; the launch traced here: 195 us
  waiting for transfers between devices  130 us (66%)
  starting transfers between devices  20.3 us (10%)
  between operations  14.6 us (7%)
  other arithmetic  13.9 us (7%)
  local copies, waits for them, and re-layouts  7.33 us (4%)
  blocking collectives  4.58 us (2%)
  matrix products  4.43 us (2%)
    reduce_scatter x1, waiting for transfers between devices, on_device(): lax.psum_scatter(transpose_dot(stacked, pre_grad), 'dom', scatter_dimensi...  62.2 us
    ppermute x15, waiting for transfers between devices, return_all_the_matrix(): jax.lax.ppermute(seen_now, row_axis, [(dd, (dd + it) % v1) for dd in rang...  38.3 us
    psum x1, waiting for transfers between devices, on_device(): summed = lax.psum(shard.astype(jnp.bfloat16), 'group')  21.2 us
    ppermute x15, starting transfers between devices, return_all_the_matrix(): jax.lax.ppermute(seen_now, row_axis, [(dd, (dd + it) % v1) for dd in rang...  12.7 us
    reduce_scatter x1, waiting for transfers between devices, on_device(): lax.psum_scatter((score_factor * transpose_dot(dscore, queries)).astype(j...  8.53 us
    all_to_all x1, starting transfers between devices, on_device(): lax.all_to_all(flags, 'dom', split_axis=0, concat_axis=0, tiled=True)  7.41 us
    all_gather x1, blocking collectives, on_device(): all_negs = lax.all_gather(own_negs, 'group', axis=0, tiled=True)  4.58 us
  transfers between devices with their start and end apart: 19, of which 13 were waited for; matrix products, arithmetic and copies ran while one was open for 6% of the time, Pallas kernels for 0%

profile of v1, /device:TPU:0, one launch (start us, length us, event | category | flops | bytes accessed | tf_op | source)
XLA Modules:
  0.0 195.4 jit_solution(13757445732330636953)
XLA Ops:
  7.2 0.0 copy-start
  7.2 0.0 copy-start.2
  7.3 1.4 compare_convert_fusion
  8.7 7.4 %all-to-all-start = ((bf16[16,1,16]{2,1,0:T(2,128)(2,1)}), bf16[16,1,16]{2,1,0:T(2,128)(2,1)S(1)}, u32[]{:S(2)}, u32[]{:S(2)}) async-start(bf16[16,1,16]{2,1,0:T(2,128)(2,1)} %compare_convert_fusion), calls=%async_computation | async-start | bytes 16384 | tf_op jit(solution)/shard_map/all_to_all | solution.py:91
  16.1 0.0 reduce-scatter.3.cloned.1.call-start
  16.2 0.7 compare_select_fusion
  16.9 0.1 reshape.332
  17.0 2.2 %gather_fusion.1 = bf16[256,512]{1,0:T(8,128)(2,1)S(1)} fusion(bf16[256,512]{1,0:T(8,128)(2,1)} %param.11, s32[1024]{0:T(1024)S(1)} %pad_clamp_fusion.2), kind=kCustom, calls=%fused_computation.1 | custom fusion | bytes 525312 | tf_op jit(solution)/shard_map/gather | solution.py:85
  19.2 0.5 collective-permute-start
  19.7 0.1 reshape.324
  19.8 0.1 reshape_squeeze.3
  19.9 0.1 convert_reduce_fusion
  20.1 0.3 fusion.19
  20.4 0.6 gather_fusion
  21.0 0.3 fusion.9
  21.7 3.4 %collective-permute-done = bf16[1,1,16,512]{3,2,1,0:T(8,128)(2,1)S(1)} collective-permute-done((bf16[1,1,16,512]{3,2,1,0:T(8,128)(2,1)S(1)}, bf16[1,1,16,512]{3,2,1,0:T(8,128)(2,1)S(1)}, u32[]{:S(2)}, u32[]{:S(2)}) %collective-permute-start) | collective-permute-done | bytes 16416 | tf_op jit(solution)/shard_map/ppermute | solution.py:40
  25.1 0.1 collective-permute-start.1
  25.2 0.1 reshape.366
  25.3 2.3 %scatter_fusion.1 = f32[256]{0:T(256)S(1)} fusion(f32[256]{0:T(256)S(1)} %add_bitcast_fusion, s32[256]{0:T(256)S(1)} %bitcast.113, f32[256]{0:T(256)S(1)} %reshape.366), kind=kCustom, calls=%fused_computation.5 | custom fusion | flops 256 | bytes 4096 | tf_op jit(solution)/shard_map/scatter-add | solution.py:103
  27.7 2.4 %collective-permute-start.14 = (bf16[1,1,16,512]{3,2,1,0:T(8,128)(2,1)S(1)}, bf16[1,1,16,512]{3,2,1,0:T(8,128)(2,1)S(1)}, u32[]{:S(2)}, u32[]{:S(2)}) collective-permute-start(bf16[1,1,16,512]{3,2,1,0:T(8,128)(2,1)S(1)} %get-tuple-element.2), channel_id=1, source_target_pairs={{0,15},{1,0},{2,1},{3,2},{4,3},{5,4},{6,5},{7,6},{8,7},{9,8},{10,9... | collective-permute-start | bytes 49160 | tf_op jit(solution)/shard_map/ppermute | solution.py:40
  30.1 2.4 %collective-permute-start.13 = (bf16[1,1,16,512]{3,2,1,0:T(8,128)(2,1)S(1)}, bf16[1,1,16,512]{3,2,1,0:T(8,128)(2,1)S(1)}, u32[]{:S(2)}, u32[]{:S(2)}) collective-permute-start(bf16[1,1,16,512]{3,2,1,0:T(8,128)(2,1)S(1)} %get-tuple-element.3), channel_id=1, source_target_pairs={{0,14},{1,15},{2,0},{3,1},{4,2},{5,3},{6,4},{7,5},{8,6},{9,7},{10,... | collective-permute-start | bytes 49160 | tf_op jit(solution)/shard_map/ppermute | solution.py:40
  32.5 0.0 collective-permute-start.12
  32.5 0.5 collective-permute-start.11
  32.9 0.0 collective-permute-done.1
  32.9 1.3 collective-permute-start.2
  34.2 3.7 %collective-permute-done.2 = bf16[1,1,16,512]{3,2,1,0:T(8,128)(2,1)S(1)} collective-permute-done((bf16[1,1,16,512]{3,2,1,0:T(8,128)(2,1)S(1)}, bf16[1,1,16,512]{3,2,1,0:T(8,128)(2,1)S(1)}, u32[]{:S(2)}, u32[]{:S(2)}) %collective-permute-start.2) | collective-permute-done | bytes 16416 | tf_op jit(solution)/shard_map/ppermute | solution.py:40
  37.9 5.5 %collective-permute-done.3 = bf16[1,1,16,512]{3,2,1,0:T(8,128)(2,1)S(1)} collective-permute-done((bf16[1,1,16,512]{3,2,1,0:T(8,128)(2,1)S(1)}, bf16[1,1,16,512]{3,2,1,0:T(8,128)(2,1)S(1)}, u32[]{:S(2)}, u32[]{:S(2)}) %collective-permute-start.3) | collective-permute-done | bytes 16416 | tf_op jit(solution)/shard_map/ppermute | solution.py:40
  43.5 5.0 %collective-permute-done.4 = bf16[1,1,16,512]{3,2,1,0:T(8,128)(2,1)S(1)} collective-permute-done((bf16[1,1,16,512]{3,2,1,0:T(8,128)(2,1)S(1)}, bf16[1,1,16,512]{3,2,1,0:T(8,128)(2,1)S(1)}, u32[]{:S(2)}, u32[]{:S(2)}) %collective-permute-start.4) | collective-permute-done | bytes 16416 | tf_op jit(solution)/shard_map/ppermute | solution.py:40
  48.4 5.5 %collective-permute-done.5 = bf16[1,1,16,512]{3,2,1,0:T(8,128)(2,1)S(1)} collective-permute-done((bf16[1,1,16,512]{3,2,1,0:T(8,128)(2,1)S(1)}, bf16[1,1,16,512]{3,2,1,0:T(8,128)(2,1)S(1)}, u32[]{:S(2)}, u32[]{:S(2)}) %collective-permute-start.5) | collective-permute-done | bytes 16416 | tf_op jit(solution)/shard_map/ppermute | solution.py:40
  54.0 4.1 %collective-permute-done.6 = bf16[1,1,16,512]{3,2,1,0:T(8,128)(2,1)S(1)} collective-permute-done((bf16[1,1,16,512]{3,2,1,0:T(8,128)(2,1)S(1)}, bf16[1,1,16,512]{3,2,1,0:T(8,128)(2,1)S(1)}, u32[]{:S(2)}, u32[]{:S(2)}) %collective-permute-start.6) | collective-permute-done | bytes 16416 | tf_op jit(solution)/shard_map/ppermute | solution.py:40
  58.0 0.1 collective-permute-start.7
  58.1 4.6 %collective-permute-done.7 = bf16[1,1,16,512]{3,2,1,0:T(8,128)(2,1)S(1)} collective-permute-done((bf16[1,1,16,512]{3,2,1,0:T(8,128)(2,1)S(1)}, bf16[1,1,16,512]{3,2,1,0:T(8,128)(2,1)S(1)}, u32[]{:S(2)}, u32[]{:S(2)}) %collective-permute-start.7) | collective-permute-done | bytes 16416 | tf_op jit(solution)/shard_map/ppermute | solution.py:40
  62.6 0.7 collective-permute-start.8
  63.4 3.3 %collective-permute-done.8 = bf16[1,1,16,512]{3,2,1,0:T(8,128)(2,1)S(1)} collective-permute-done((bf16[1,1,16,512]{3,2,1,0:T(8,128)(2,1)S(1)}, bf16[1,1,16,512]{3,2,1,0:T(8,128)(2,1)S(1)}, u32[]{:S(2)}, u32[]{:S(2)}) %collective-permute-start.8) | collective-permute-done | bytes 16416 | tf_op jit(solution)/shard_map/ppermute | solution.py:40
  66.7 2.8 %collective-permute-start.9 = (bf16[1,1,16,512]{3,2,1,0:T(8,128)(2,1)S(1)}, bf16[1,1,16,512]{3,2,1,0:T(8,128)(2,1)S(1)}, u32[]{:S(2)}, u32[]{:S(2)}) collective-permute-start(bf16[1,1,16,512]{3,2,1,0:T(8,128)(2,1)S(1)} %get-tuple-element.7), channel_id=1, source_target_pairs={{0,10},{1,11},{2,12},{3,13},{4,14},{5,15},{6,0},{7,1},{8,2},{9,3},... | collective-permute-start | bytes 49160 | tf_op jit(solution)/shard_map/ppermute | solution.py:40
  69.5 1.9 collective-permute-done.9
  71.3 2.1 %collective-permute-start.10 = (bf16[1,1,16,512]{3,2,1,0:T(8,128)(2,1)S(1)}, bf16[1,1,16,512]{3,2,1,0:T(8,128)(2,1)S(1)}, u32[]{:S(2)}, u32[]{:S(2)}) collective-permute-start(bf16[1,1,16,512]{3,2,1,0:T(8,128)(2,1)S(1)} %get-tuple-element.6), channel_id=1, source_target_pairs={{0,11},{1,12},{2,13},{3,14},{4,15},{5,0},{6,1},{7,2},{8,3},{9,4},{... | collective-permute-start | bytes 49160 | tf_op jit(solution)/shard_map/ppermute | solution.py:40
  73.4 1.4 collective-permute-done.10
  74.9 0.1 convert_multiply_fusion
  75.1 2.3 %scatter_fusion = f32[256,512]{1,0:T(8,128)S(1)} fusion(f32[256,512]{1,0:T(8,128)S(1)} %bitcast.106, s32[256]{0:T(256)S(1)} %bitcast.114, f32[256,512]{1,0:T(8,128)S(1)} %bitcast.111), kind=kCustom, calls=%fused_computation.4 | custom fusion | flops 131072 | bytes 1573888 | tf_op jit(solution)/shard_map/scatter-add | solution.py:102
  77.4 0.1 divide_convert_fusion
  77.5 0.4 multiply_reduce_fusion.1
  77.9 0.1 multiply_convert_fusion
  78.0 0.0 copy-start.1
  78.0 0.6 gather_fusion.3
  78.7 4.6 %all-gather = bf16[64,512]{1,0:T(8,128)(2,1)S(1)} all-gather(bf16[32,512]{1,0:T(8,128)(2,1)S(1)} %gather_fusion.3), channel_id=2, replica_groups=mesh['group'=2,'dom'=16] {'group'}, dimensions={0}, use_global_device_ids=true | all-gather | bytes 98304 | tf_op jit(solution)/shard_map/all_gather | solution.py:117
  83.2 2.0 %gather_fusion.2 = bf16[512,512]{1,0:T(8,128)(2,1)S(1)} fusion(bf16[256,512]{1,0:T(8,128)(2,1)S(1)} %multiply_convert_fusion, s32[1024]{0:T(1024)S(1)} %pad_clamp_fusion.1), kind=kCustom, calls=%fused_computation.2 | custom fusion | bytes 1050624 | tf_op jit(solution)/shard_map/gather | solution.py:111
  85.2 0.3 multiply_convert_fusion.1
  85.6 0.8 fusion.4
  86.4 0.0 reduce-scatter.3.cloned.1.call-update
  86.4 0.0 reduce-scatter.5.cloned.1.call-start
  86.5 0.3 convolution_multiply_fusion
  86.8 3.7 %scatter_custom_fusion.2 = f32[256,512]{1,0:T(8,128)S(1)} fusion(s32[512]{0:T(512)S(1)} %bitcast.116, f32[512,512]{1,0:T(8,128)S(1)} %convolution_multiply_fusion, f32[]{:T(128)} %constant.267.clone.1), kind=kCustom, calls=%fused_computation.31 | custom fusion | flops 262144 | bytes 524292 | tf_op jit(solution)/shard_map/scatter-add | solution.py:129
  90.5 8.5 %reduce-scatter.3.cloned.1.call-done = bf16[32,512]{1,0:T(8,128)(2,1)} async-done(((bf16[64,512]{1,0:T(8,128)(2,1)}), bf16[32,512]{1,0:T(8,128)(2,1)}) %reduce-scatter.3.cloned.1.call-update) | async-done | bytes 32784 | tf_op jit(solution)/shard_map/reduce_scatter | solution.py:122
  99.1 1.2 scatter_custom_fusion.3
  100.3 0.1 multiply_reduce_fusion
  100.4 2.0 fusion.5
  102.4 0.0 reduce-scatter.5.cloned.1.call-update
  102.4 0.0 all-reduce.2.cloned.1.call-start
  102.5 62.2 %reduce-scatter.5.cloned.1.call-done = f32[64,512]{1,0:T(8,128)} async-done(((f32[1024,512]{1,0:T(8,128)}), f32[64,512]{1,0:T(8,128)}) %reduce-scatter.5.cloned.1.call-update) | async-done | bytes 131088 | tf_op jit(solution)/shard_map/reduce_scatter | solution.py:134
  164.6 1.5 convert_element_type.66
  166.2 0.0 all-reduce.2.cloned.1.call-update
  166.2 21.2 %all-reduce.2.cloned.1.call-done = bf16[64,512]{1,0:T(8,128)(2,1)} async-done(((bf16[64,512]{1,0:T(8,128)(2,1)}), bf16[64,512]{1,0:T(8,128)(2,1)}) %all-reduce.2.cloned.1.call-update) | async-done | bytes 65552 | tf_op jit(solution)/shard_map/psum | solution.py:137
  187.4 1.5 copy.33
  (55 shorter events, 0.2 us)
Async XLA Ops:
  7.2 70.3 %copy-start = (bf16[512,512]{1,0:T(8,128)(2,1)S(1)}, bf16[512,512]{1,0:T(8,128)(2,1)}, u32[]{:S(2)}) copy-start(bf16[512,512]{1,0:T(8,128)(2,1)} %param.21) | copy-start | bytes 1572868
  7.2 12.9 %copy-start.2 = (bf16[256,512]{1,0:T(8,128)(2,1)S(1)}, bf16[256,512]{1,0:T(8,128)(2,1)}, u32[]{:S(2)}) copy-start(bf16[256,512]{1,0:T(8,128)(2,1)} %param.11) | copy-start | bytes 786436
  7.2 12.5 %copy-start.9 = (s32[1,32]{1,0:T(1,128)S(1)}, s32[1,32]{1,0:T(1,128)}, u32[]{:S(2)}) copy-start(s32[1,32]{1,0:T(1,128)} %param.19) | copy-start | bytes 388
  7.2 12.5 %copy-start.7 = (s32[1,2,4]{2,1,0:T(2,128)S(1)}, s32[1,2,4]{2,1,0:T(2,128)}, u32[]{:S(2)}) copy-start(s32[1,2,4]{2,1,0:T(2,128)} %param.12) | copy-start | bytes 100
  7.2 12.5 %copy-start.5 = (s32[1,16,16]{2,1,0:T(8,128)S(1)}, s32[1,16,16]{2,1,0:T(8,128)}, u32[]{:S(2)}) copy-start(s32[1,16,16]{2,1,0:T(8,128)} %param.16) | copy-start | bytes 3076
  7.2 12.6 %copy-start.3 = (bf16[1,2,4,128,128]{4,3,2,1,0:T(8,128)(2,1)S(1)}, bf16[1,2,4,128,128]{4,3,2,1,0:T(8,128)(2,1)}, u32[]{:S(2)}) copy-start(bf16[1,2,4,128,128]{4,3,2,1,0:T(8,128)(2,1)} %param.13) | copy-start | bytes 786436
  7.2 12.8 %copy-start.6 = (s32[1,512]{1,0:T(1,128)S(1)}, s32[1,512]{1,0:T(1,128)}, u32[]{:S(2)}) copy-start(s32[1,512]{1,0:T(1,128)} %param.17) | copy-start | bytes 6148
  7.2 12.8 %copy-start.4 = (bf16[512,512]{1,0:T(8,128)(2,1)S(1)}, bf16[512,512]{1,0:T(8,128)(2,1)}, u32[]{:S(2)}) copy-start(bf16[512,512]{1,0:T(8,128)(2,1)} %param.20) | copy-start | bytes 1572868
  8.7 16.5 %all-to-all-start = ((bf16[16,1,16]{2,1,0:T(2,128)(2,1)}), bf16[16,1,16]{2,1,0:T(2,128)(2,1)S(1)}, u32[]{:S(2)}, u32[]{:S(2)}) async-start(bf16[16,1,16]{2,1,0:T(2,128)(2,1)} %compare_convert_fusion), calls=%async_computation | async-start | bytes 16384 | tf_op jit(solution)/shard_map/all_to_all | solution.py:91
  16.1 82.9 %reduce-scatter.3.cloned.1.call-start = ((), (), s32[]{:S(2)}) async-start(), calls=%async_computation.3 | async-start | bytes 98304 | tf_op jit(solution)/shard_map/reduce_scatter | solution.py:122
  19.2 5.9 %collective-permute-start = (bf16[1,1,16,512]{3,2,1,0:T(8,128)(2,1)S(1)}, bf16[1,1,16,512]{3,2,1,0:T(8,128)(2,1)S(1)}, u32[]{:S(2)}, u32[]{:S(2)}) collective-permute-start(bf16[1,1,16,512]{3,2,1,0:T(8,128)(2,1)S(1)} %dynamic-slice_bitcast_fusion.14), channel_id=1, source_target_pairs={{0,1},{1,2},{2,3},{3,4},{4,5},{5,6},{6,7},{7,8},{8,9},{9,10},{10,1... | collective-permute-start | bytes 49160 | tf_op jit(solution)/shard_map/ppermute | solution.py:40
  25.1 7.8 %collective-permute-start.1 = (bf16[1,1,16,512]{3,2,1,0:T(8,128)(2,1)S(1)}, bf16[1,1,16,512]{3,2,1,0:T(8,128)(2,1)S(1)}, u32[]{:S(2)}, u32[]{:S(2)}) collective-permute-start(bf16[1,1,16,512]{3,2,1,0:T(8,128)(2,1)S(1)} %get-tuple-element.15), channel_id=1, source_target_pairs={{0,2},{1,3},{2,4},{3,5},{4,6},{5,7},{6,8},{7,9},{8,10},{9,11},{10,... | collective-permute-start | bytes 49160 | tf_op jit(solution)/shard_map/ppermute | solution.py:40
  27.7 47.3 %collective-permute-start.14 = (bf16[1,1,16,512]{3,2,1,0:T(8,128)(2,1)S(1)}, bf16[1,1,16,512]{3,2,1,0:T(8,128)(2,1)S(1)}, u32[]{:S(2)}, u32[]{:S(2)}) collective-permute-start(bf16[1,1,16,512]{3,2,1,0:T(8,128)(2,1)S(1)} %get-tuple-element.2), channel_id=1, source_target_pairs={{0,15},{1,0},{2,1},{3,2},{4,3},{5,4},{6,5},{7,6},{8,7},{9,8},{10,9... | collective-permute-start | bytes 49160 | tf_op jit(solution)/shard_map/ppermute | solution.py:40
  30.1 44.8 %collective-permute-start.13 = (bf16[1,1,16,512]{3,2,1,0:T(8,128)(2,1)S(1)}, bf16[1,1,16,512]{3,2,1,0:T(8,128)(2,1)S(1)}, u32[]{:S(2)}, u32[]{:S(2)}) collective-permute-start(bf16[1,1,16,512]{3,2,1,0:T(8,128)(2,1)S(1)} %get-tuple-element.3), channel_id=1, source_target_pairs={{0,14},{1,15},{2,0},{3,1},{4,2},{5,3},{6,4},{7,5},{8,6},{9,7},{10,... | collective-permute-start | bytes 49160 | tf_op jit(solution)/shard_map/ppermute | solution.py:40
  32.5 42.4 %collective-permute-start.12 = (bf16[1,1,16,512]{3,2,1,0:T(8,128)(2,1)S(1)}, bf16[1,1,16,512]{3,2,1,0:T(8,128)(2,1)S(1)}, u32[]{:S(2)}, u32[]{:S(2)}) collective-permute-start(bf16[1,1,16,512]{3,2,1,0:T(8,128)(2,1)S(1)} %get-tuple-element.4), channel_id=1, source_target_pairs={{0,13},{1,14},{2,15},{3,0},{4,1},{5,2},{6,3},{7,4},{8,5},{9,6},{10... | collective-permute-start | bytes 49160 | tf_op jit(solution)/shard_map/ppermute | solution.py:40
  32.5 42.4 %collective-permute-start.11 = (bf16[1,1,16,512]{3,2,1,0:T(8,128)(2,1)S(1)}, bf16[1,1,16,512]{3,2,1,0:T(8,128)(2,1)S(1)}, u32[]{:S(2)}, u32[]{:S(2)}) collective-permute-start(bf16[1,1,16,512]{3,2,1,0:T(8,128)(2,1)S(1)} %get-tuple-element.5), channel_id=1, source_target_pairs={{0,12},{1,13},{2,14},{3,15},{4,0},{5,1},{6,2},{7,3},{8,4},{9,5},{1... | collective-permute-start | bytes 49160 | tf_op jit(solution)/shard_map/ppermute | solution.py:40
  32.9 5.0 %collective-permute-start.2 = (bf16[1,1,16,512]{3,2,1,0:T(8,128)(2,1)S(1)}, bf16[1,1,16,512]{3,2,1,0:T(8,128)(2,1)S(1)}, u32[]{:S(2)}, u32[]{:S(2)}) collective-permute-start(bf16[1,1,16,512]{3,2,1,0:T(8,128)(2,1)S(1)} %get-tuple-element.14), channel_id=1, source_target_pairs={{0,3},{1,4},{2,5},{3,6},{4,7},{5,8},{6,9},{7,10},{8,11},{9,12},{10... | collective-permute-start | bytes 49160 | tf_op jit(solution)/shard_map/ppermute | solution.py:40
  37.9 5.5 %collective-permute-start.3 = (bf16[1,1,16,512]{3,2,1,0:T(8,128)(2,1)S(1)}, bf16[1,1,16,512]{3,2,1,0:T(8,128)(2,1)S(1)}, u32[]{:S(2)}, u32[]{:S(2)}) collective-permute-start(bf16[1,1,16,512]{3,2,1,0:T(8,128)(2,1)S(1)} %get-tuple-element.13), channel_id=1, source_target_pairs={{0,4},{1,5},{2,6},{3,7},{4,8},{5,9},{6,10},{7,11},{8,12},{9,13},{1... | collective-permute-start | bytes 49160 | tf_op jit(solution)/shard_map/ppermute | solution.py:40
  43.4 5.0 %collective-permute-start.4 = (bf16[1,1,16,512]{3,2,1,0:T(8,128)(2,1)S(1)}, bf16[1,1,16,512]{3,2,1,0:T(8,128)(2,1)S(1)}, u32[]{:S(2)}, u32[]{:S(2)}) collective-permute-start(bf16[1,1,16,512]{3,2,1,0:T(8,128)(2,1)S(1)} %get-tuple-element.12), channel_id=1, source_target_pairs={{0,5},{1,6},{2,7},{3,8},{4,9},{5,10},{6,11},{7,12},{8,13},{9,14},{... | collective-permute-start | bytes 49160 | tf_op jit(solution)/shard_map/ppermute | solution.py:40
  48.4 5.5 %collective-permute-start.5 = (bf16[1,1,16,512]{3,2,1,0:T(8,128)(2,1)S(1)}, bf16[1,1,16,512]{3,2,1,0:T(8,128)(2,1)S(1)}, u32[]{:S(2)}, u32[]{:S(2)}) collective-permute-start(bf16[1,1,16,512]{3,2,1,0:T(8,128)(2,1)S(1)} %get-tuple-element.11), channel_id=1, source_target_pairs={{0,6},{1,7},{2,8},{3,9},{4,10},{5,11},{6,12},{7,13},{8,14},{9,15},... | collective-permute-start | bytes 49160 | tf_op jit(solution)/shard_map/ppermute | solution.py:40
  53.9 4.1 %collective-permute-start.6 = (bf16[1,1,16,512]{3,2,1,0:T(8,128)(2,1)S(1)}, bf16[1,1,16,512]{3,2,1,0:T(8,128)(2,1)S(1)}, u32[]{:S(2)}, u32[]{:S(2)}) collective-permute-start(bf16[1,1,16,512]{3,2,1,0:T(8,128)(2,1)S(1)} %get-tuple-element.10), channel_id=1, source_target_pairs={{0,7},{1,8},{2,9},{3,10},{4,11},{5,12},{6,13},{7,14},{8,15},{9,0},... | collective-permute-start | bytes 49160 | tf_op jit(solution)/shard_map/ppermute | solution.py:40
  58.0 4.6 %collective-permute-start.7 = (bf16[1,1,16,512]{3,2,1,0:T(8,128)(2,1)S(1)}, bf16[1,1,16,512]{3,2,1,0:T(8,128)(2,1)S(1)}, u32[]{:S(2)}, u32[]{:S(2)}) collective-permute-start(bf16[1,1,16,512]{3,2,1,0:T(8,128)(2,1)S(1)} %get-tuple-element.9), channel_id=1, source_target_pairs={{0,8},{1,9},{2,10},{3,11},{4,12},{5,13},{6,14},{7,15},{8,0},{9,1},... | collective-permute-start | bytes 49160 | tf_op jit(solution)/shard_map/ppermute | solution.py:40
  62.6 4.1 %collective-permute-start.8 = (bf16[1,1,16,512]{3,2,1,0:T(8,128)(2,1)S(1)}, bf16[1,1,16,512]{3,2,1,0:T(8,128)(2,1)S(1)}, u32[]{:S(2)}, u32[]{:S(2)}) collective-permute-start(bf16[1,1,16,512]{3,2,1,0:T(8,128)(2,1)S(1)} %get-tuple-element.8), channel_id=1, source_target_pairs={{0,9},{1,10},{2,11},{3,12},{4,13},{5,14},{6,15},{7,0},{8,1},{9,2},... | collective-permute-start | bytes 49160 | tf_op jit(solution)/shard_map/ppermute | solution.py:40
  66.7 4.6 %collective-permute-start.9 = (bf16[1,1,16,512]{3,2,1,0:T(8,128)(2,1)S(1)}, bf16[1,1,16,512]{3,2,1,0:T(8,128)(2,1)S(1)}, u32[]{:S(2)}, u32[]{:S(2)}) collective-permute-start(bf16[1,1,16,512]{3,2,1,0:T(8,128)(2,1)S(1)} %get-tuple-element.7), channel_id=1, source_target_pairs={{0,10},{1,11},{2,12},{3,13},{4,14},{5,15},{6,0},{7,1},{8,2},{9,3},... | collective-permute-start | bytes 49160 | tf_op jit(solution)/shard_map/ppermute | solution.py:40
  71.3 3.5 %collective-permute-start.10 = (bf16[1,1,16,512]{3,2,1,0:T(8,128)(2,1)S(1)}, bf16[1,1,16,512]{3,2,1,0:T(8,128)(2,1)S(1)}, u32[]{:S(2)}, u32[]{:S(2)}) collective-permute-start(bf16[1,1,16,512]{3,2,1,0:T(8,128)(2,1)S(1)} %get-tuple-element.6), channel_id=1, source_target_pairs={{0,11},{1,12},{2,13},{3,14},{4,15},{5,0},{6,1},{7,2},{8,3},{9,4},{... | collective-permute-start | bytes 49160 | tf_op jit(solution)/shard_map/ppermute | solution.py:40
  78.0 7.2 %copy-start.1 = (bf16[256,512]{1,0:T(8,128)(2,1)}, bf16[256,512]{1,0:T(8,128)(2,1)S(1)}, u32[]{:S(2)}) copy-start(bf16[256,512]{1,0:T(8,128)(2,1)S(1)} %multiply_convert_fusion) | copy-start | bytes 786436
  83.2 2.0 %copy-start.8 = (s32[1,512]{1,0:T(1,128)S(1)}, s32[1,512]{1,0:T(1,128)}, u32[]{:S(2)}) copy-start(s32[1,512]{1,0:T(1,128)} %param.18) | copy-start | bytes 6148
  86.4 78.2 %reduce-scatter.5.cloned.1.call-start = ((), (), s32[]{:S(2)}) async-start(), calls=%async_computation.4 | async-start | bytes 2228224 | tf_op jit(solution)/shard_map/reduce_scatter | solution.py:134
  102.4 85.0 %all-reduce.2.cloned.1.call-start = ((), (), s32[]{:S(2)}) async-start(), calls=%async_computation.5 | async-start | bytes 131072 | tf_op jit(solution)/shard_map/psum | solution.py:137
Sparse Core Ops, SparseCore 0:
  86.6 12.4 reduce-scatter.2
  102.8 61.7 reduce-scatter.4
  167.4 19.8 all-reduce.1
